TPU v7x, 32 devices: a whole 2x2x4 slice. The times are simulated.
32 devices in a mesh: nodes: 8 (over z, x), dp: 4 (over y, core).
Axes of the slice: x: 2, y: 2, z: 4, core: 2. Of those that a mesh axis runs over, the one named last changes fastest.
Arguments:
- samples: float32 [16384, 256], P('dp'), may hold values from -96 to 96, as said below
- basis_matrix: float32 [8192, 4096], P('nodes', 'dp'), may hold values from 0 to 0.03
- weights: float32 [4096, 256], P('dp'), may hold values from -12 to 12, as said below
Outputs:
- new_weights: float32 [4096, 256], P('dp')
- new_centres: float32 [8192, 256], P('nodes')
Inputs may be any that keep to these rules, and one draw needn't show every extreme that they name: `samples`: finite data values. `weights`: finite weight values.
All inputs are finite; a program needn't handle non-finite values.
Results may differ from a plain program's by a relative error of at most 0.0003.
Values sent between devices are 32-bit elements; how exact they have to be, the bound alone decides.
A program may use at most 64 MiB of HBM per device.

v0:
```python
import math

import jax
import jax.numpy as jnp
from jax import lax
from jax.sharding import PartitionSpec as P

highest = lax.Precision.HIGHEST
inverse_temp = 0.25
shrink = 0.95


def merged_2(part, axis, combine):
    gathered = jax.tree.map(lambda a: lax.all_gather(a, axis), part)

    def take(source):
        return jax.tree.map(lambda a: lax.dynamic_index_in_dim(a, source, 0, False), gathered)

    return lax.fori_loop(
        1, lax.axis_size(axis), lambda source, state: combine(state, take(source)), take(0)
    )


def combine(first, second):
    merged = jnp.maximum(first[0], second[0])
    return (merged, first[1] * jnp.exp(first[0] - merged) + second[1] * jnp.exp(second[0] - merged))


def body(samples, basis_matrix, weights):
    node_count = basis_matrix.shape[0] * lax.axis_size("nodes")
    vector_count = samples.shape[0] * lax.axis_size("dp")
    partial_centres = jnp.dot(
        basis_matrix, weights, precision=highest, preferred_element_type=jnp.float32
    )
    centres = lax.psum(partial_centres, "dp")
    cross = lax.dot_general(
        centres,
        samples,
        (((1,), (1,)), ((), ())),
        precision=highest,
        preferred_element_type=jnp.float32,
    )
    scores = inverse_temp * (cross - 0.5 * jnp.sum(centres * centres, axis=1)[:, None])
    local_max = jnp.max(scores, axis=0)
    exponent = jnp.exp(scores - local_max[None, :])
    maxima, totals = merged_2((local_max, jnp.sum(exponent, axis=0)), "nodes", combine)
    resp = exponent * (jnp.exp(local_max - maxima) / totals)[None, :]
    weighted = jnp.dot(resp, samples, precision=highest, preferred_element_type=jnp.float32)
    local_terms = jnp.sum(resp, axis=1)[:, None] * centres - weighted
    node_terms = lax.psum(local_terms, "dp")
    partial_gradient = lax.dot_general(
        basis_matrix,
        node_terms,
        (((0,), (0,)), ((), ())),
        precision=highest,
        preferred_element_type=jnp.float32,
    )
    step_rate = 8.0 * math.sqrt(node_count) / vector_count
    gradient = lax.psum(partial_gradient, "nodes")
    new_weights = shrink * weights - step_rate * gradient
    partial_new = jnp.dot(
        basis_matrix, new_weights, precision=highest, preferred_element_type=jnp.float32
    )
    new_centres = lax.psum(partial_new, "dp")
    return (new_weights, new_centres)


def solution(mesh):
    in_specs = (P("dp", None), P("nodes", "dp"), P("dp", None))
    out_specs = (P("dp", None), P("nodes", None))
    return jax.shard_map(body, mesh=mesh, in_specs=in_specs, out_specs=out_specs, check_vma=False)
```

profile of v0, /device:TPU:1, one launch (start us, length us, event | category | flops | bytes accessed | tf_op | source)
XLA Modules:
  0.0 349.8 jit_solution(18118655665479048383)
XLA Ops:
  7.2 0.0 all-reduce.5.cloned.1.call-start
  7.2 6.9 %fusion.12 = f32[1024,256]{1,0:T(8,128)} fusion(f32[1024,1024]{1,0:T(8,128)} %param.6, f32[1024,256]{1,0:T(8,128)} %param.7), kind=kOutput, calls=%fused_computation.22 | convolution fusion | flops 3221225472 | bytes 6291456 | tf_op jit(solution)/shard_map/dot_general | solution.py:32
  14.1 0.0 all-reduce.5.cloned.1.call-update
  14.1 0.0 all-reduce.7.cloned.1.call-start
  14.2 38.1 %all-reduce.5.cloned.1.call-done = f32[1024,256]{1,0:T(8,128)} async-done(((f32[1024,256]{1,0:T(8,128)}), f32[1024,256]{1,0:T(8,128)}) %all-reduce.5.cloned.1.call-update) | async-done | bytes 1048592 | tf_op jit(solution)/shard_map/psum | solution.py:35
  52.3 1.4 multiply_reduce_fusion.1
  53.7 17.0 %fusion.2 = (f32[4096]{0:T(1024)S(1)}, f32[1024,4096]{1,0:T(8,128)S(1)}) fusion(f32[1024]{0:T(1024)S(1)} %broadcast_multiply_fusion, f32[1024,256]{1,0:T(8,128)} %all-reduce.5.cloned.1.call-done, f32[4096,256]{1,0:T(8,128)} %param.5), kind=kOutput, calls=%fused_computation.8 | convolution fusion | flops 12897480704 | bytes 22040576 | tf_op jit(solution)/shard_map/dot_general | solution.py:36
  70.7 0.0 copy-start
  70.7 5.7 %copy-done = f32[1024,4096]{1,0:T(8,128)} copy-done((f32[1024,4096]{1,0:T(8,128)}, f32[1024,4096]{1,0:T(8,128)S(1)}, u32[]{:S(2)}) %copy-start) | copy-done | bytes 16777240
  76.4 3.8 %fusion.3 = f32[4096]{0:T(1024)S(1)} fusion(f32[1024,4096]{1,0:T(8,128)S(1)} %get-tuple-element.156, f32[4096]{0:T(1024)S(1)} %get-tuple-element.155, f32[1024]{0:T(1024)S(1)} %broadcast_multiply_fusion), kind=kLoop, calls=%fused_computation.9 | loop fusion | flops 16773120 | bytes 16814080 | tf_op jit(solution)/shard_map/reduce_sum | solution.py:46
  80.2 24.2 %all-gather.1 = f32[32768]{0:T(1024)S(1)} all-gather(f32[4096]{0:T(1024)S(1)} %fusion.3), channel_id=3, replica_groups=mesh['nodes'=8,'dp'=4] {'nodes'}, dimensions={0}, use_global_device_ids=true | all-gather | bytes 147456 | tf_op jit(solution)/shard_map/all_gather | solution.py:14
  104.4 24.4 %all-gather = f32[32768]{0:T(1024)S(1)} all-gather(f32[4096]{0:T(1024)S(1)} %get-tuple-element.155), channel_id=2, replica_groups=mesh['nodes'=8,'dp'=4] {'nodes'}, dimensions={0}, use_global_device_ids=true | all-gather | bytes 147456 | tf_op jit(solution)/shard_map/all_gather | solution.py:14
  128.9 0.6 while.17
  129.5 0.0 copy-start.1
  129.5 9.5 %multiply_reduce_fusion = f32[1024]{0:T(1024)S(1)} fusion(f32[1024,4096]{1,0:T(8,128)} %copy-done, f32[4096]{0:T(1024)S(1)} %exponential_divide_fusion, f32[4096]{0:T(1024)S(1)} %get-tuple-element.155, f32[1024]{0:T(1024)S(1)} %broadcast_multiply_fusion), kind=kLoop, calls=%fused_computation.7 | loop fusion | flops 20970496 | bytes 16818176 | tf_op jit(solution)/shard_map/reduce_sum | solution.py:49
  139.0 0.0 copy-done.2
  139.0 1.2 copy-done.1
  140.1 20.6 %fusion.8 = f32[1024,256]{1,0:T(8,128)} fusion(f32[4096,256]{1,0:T(8,128)} %param.5, f32[1024,4096]{1,0:T(8,128)S(1)} %copy-done.1, f32[4096]{0:T(1024)S(1)} %exponential_divide_fusion, f32[4096]{0:T(1024)S(1)} %get-tuple-element.155, f32[1024]{0:T(1024)S(1)} %broadcast_multiply_fusion, f32[1024,256]{1,0:T(8,128)S(1)} %copy-done.2, ...), kind=kOutput, calls=%fused_computation.16 | convolution fusion | flops 12902203392 | bytes 23109632 | tf_op jit(solution)/shard_map/dot_general | solution.py:48
  160.8 0.0 all-reduce.7.cloned.1.call-update
  160.8 0.0 all-reduce.9.cloned.1.call-start
  160.9 49.5 %all-reduce.7.cloned.1.call-done = f32[1024,256]{1,0:T(8,128)} async-done(((f32[1024,256]{1,0:T(8,128)}), f32[1024,256]{1,0:T(8,128)}) %all-reduce.7.cloned.1.call-update) | async-done | bytes 1048592 | tf_op jit(solution)/shard_map/psum | solution.py:50
  210.4 7.1 %convolution_bitcast_fusion.1 = f32[1024,256]{0,1:T(8,128)} fusion(f32[1024,256]{1,0:T(8,128)} %all-reduce.7.cloned.1.call-done, f32[1024,1024]{1,0:T(8,128)} %param.6), kind=kOutput, calls=%fused_computation.15 | convolution fusion | flops 3221225472 | bytes 6291456 | tf_op jit(solution)/shard_map/dot_general | solution.py:51
  217.5 0.0 all-reduce.9.cloned.1.call-update
  217.5 0.3 all-reduce.11.cloned.1.call-start
  217.8 0.3 copy.8
  218.1 78.6 %all-reduce.9.cloned.1.call-done = f32[1024,256]{0,1:T(8,128)} async-done(((f32[1024,256]{0,1:T(8,128)}), f32[1024,256]{0,1:T(8,128)}) %all-reduce.9.cloned.1.call-update) | async-done | bytes 1048592 | tf_op jit(solution)/shard_map/psum | solution.py:59
  296.7 1.4 multiply_subtract_fusion
  298.1 6.9 %convolution_bitcast_fusion = f32[1024,256]{0,1:T(8,128)} fusion(f32[1024,256]{0,1:T(8,128)S(1)} %multiply_subtract_fusion, f32[1024,1024]{1,0:T(8,128)} %param.6), kind=kOutput, calls=%fused_computation.14 | convolution fusion | flops 3221225472 | bytes 6291456 | tf_op jit(solution)/shard_map/dot_general | solution.py:61
  305.0 0.0 all-reduce.11.cloned.1.call-update
  305.0 1.3 copy.9
  306.3 34.5 %all-reduce.11.cloned.1.call-done = f32[1024,256]{0,1:T(8,128)} async-done(((f32[1024,256]{0,1:T(8,128)}), f32[1024,256]{0,1:T(8,128)}) %all-reduce.11.cloned.1.call-update) | async-done | bytes 1048592 | tf_op jit(solution)/shard_map/psum | solution.py:64
  340.8 2.5 copy.10
  (23 shorter events, 0.4 us)
Async XLA Ops:
  7.2 45.1 %all-reduce.5.cloned.1.call-start = ((), (), s32[]{:S(2)}) async-start(), calls=%async_computation | async-start | bytes 2097152 | tf_op jit(solution)/shard_map/psum | solution.py:35
  14.1 196.3 %all-reduce.7.cloned.1.call-start = ((), (), s32[]{:S(2)}) async-start(), calls=%async_computation.1 | async-start | bytes 2097152 | tf_op jit(solution)/shard_map/psum | solution.py:50
  70.7 5.7 %copy-start = (f32[1024,4096]{1,0:T(8,128)}, f32[1024,4096]{1,0:T(8,128)S(1)}, u32[]{:S(2)}) copy-start(f32[1024,4096]{1,0:T(8,128)S(1)} %get-tuple-element.156) | copy-start | bytes 50331652
  76.4 62.5 %copy-start.2 = (f32[1024,256]{1,0:T(8,128)S(1)}, f32[1024,256]{1,0:T(8,128)}, u32[]{:S(2)}) copy-start(f32[1024,256]{1,0:T(8,128)} %all-reduce.5.cloned.1.call-done) | copy-start | bytes 3145732
  129.5 10.7 %copy-start.1 = (f32[1024,4096]{1,0:T(8,128)S(1)}, f32[1024,4096]{1,0:T(8,128)}, u32[]{:S(2)}) copy-start(f32[1024,4096]{1,0:T(8,128)} %copy-done) | copy-start | bytes 50331652
  140.1 77.6 %copy-start.3 = (f32[1024,256]{1,0:T(8,128)S(1)}, f32[1024,256]{1,0:T(8,128)}, u32[]{:S(2)}) copy-start(f32[1024,256]{1,0:T(8,128)} %param.7) | copy-start | bytes 3145732
  160.8 135.9 %all-reduce.9.cloned.1.call-start = ((), (), s32[]{:S(2)}) async-start(), calls=%async_computation.2 | async-start | bytes 2097152 | tf_op jit(solution)/shard_map/psum | solution.py:59
  217.5 123.3 %all-reduce.11.cloned.1.call-start = ((), (), s32[]{:S(2)}) async-start(), calls=%async_computation.3 | async-start | bytes 2097152 | tf_op jit(solution)/shard_map/psum | solution.py:64
Sparse Core Ops, SparseCore 0:
  14.2 37.9 all-reduce.4
  160.9 49.3 all-reduce.6
  217.6 79.0 all-reduce.8
  305.1 35.6 all-reduce.10
where the time goes:
time: 351 us; the launch traced here: 350 us
  waiting for transfers between devices  201 us (57%)
  matrix products  58.4 us (17%)
  blocking collectives  48.6 us (14%)
  other arithmetic  16.3 us (5%)
  between operations  13.9 us (4%)
  local copies, waits for them, and re-layouts  11.3 us (3%)
    psum x1, waiting for transfers between devices, body(): gradient = lax.psum(partial_gradient, 'nodes')  78.6 us
    psum x1, waiting for transfers between devices, body(): node_terms = lax.psum(local_terms, 'dp')  49.5 us
    all_gather x2, blocking collectives, merged_2(): gathered = jax.tree.map(lambda a: lax.all_gather(a, axis), part)  48.6 us
    psum x1, waiting for transfers between devices, body(): centres = lax.psum(partial_centres, 'dp')  38.1 us
    psum x1, waiting for transfers between devices, body(): new_centres = lax.psum(partial_new, 'dp')  34.5 us
    dot_general x1, matrix products, body(): jnp.dot(resp, samples, precision=highest, preferred_element_type=jnp.floa...  20.6 us
    dot_general x1, matrix products, body(): lax.dot_general(centres, samples, (((1,), (1,)), ((), ())), precision=hig...  17 us
    unnamed x11, local copies, waits for them, and re-layouts  11.1 us
  transfers between devices with their start and end apart: 4, of which 4 were waited for; matrix products, arithmetic and copies ran while one was open for 0% of the time, Pallas kernels for 0%

commit v1 on v0

v1 whole, which is shorter than its diff:
```python
import functools
import math

import jax
import jax.numpy as jnp
from jax import lax
from jax.experimental import pallas as pl
from jax.experimental.pallas import tpu as pltpu
from jax.sharding import PartitionSpec as P

f32 = jnp.float32
bf16 = jnp.bfloat16
MESH = pl.DeviceIdType.MESH
shrink = 0.95
CH = 4
VC = 512


def split(a):
    hi = a.astype(bf16)
    return hi, (a - hi.astype(f32)).astype(bf16)


def dot(a, b, trans_b=False):
    dims = (((1,), (1 if trans_b else 0,)), ((), ()))
    return lax.dot_general(a, b, dims, preferred_element_type=f32)


def dot3(ah, al, bh, bl, trans_b=False):
    return dot(ah, bh, trans_b) + (dot(ah, bl, trans_b) + dot(al, bh, trans_b))


def kernel(
    nn, nd, rate,
    x_hbm, b_hbm, w_ref, nw_hbm, nc_hbm,
    xv, bv, xh, xl, bh, bl, bth, btl, wh, wl,
    part, cent, land_c, land_y,
    bias, ex, st, st_in, fac,
    grad, lx1, lz1, lx2, lz2, nw, nc,
    lsem, ssem, rsem, st_s, st_r, g_s, g_r,
):
    kk, mm = bv.shape
    nv, d = xv.shape
    node = lax.axis_index("nodes")
    dp = lax.axis_index("dp")
    core = lax.rem(dp, 2)
    yy = dp // 2
    ny = nd // 2
    xx = lax.rem(node, 2)
    zz = node // 2
    nz = nn // 2
    tk = kk // CH
    half = tk // 2
    extra = 8

    b_cp = []
    for i in range(CH):
        rows = pl.ds(i * tk, tk)
        cp = pltpu.make_async_copy(b_hbm.at[rows], bv.at[rows], lsem.at[i])
        cp.start()
        b_cp.append(cp)
    x_cp = pltpu.make_async_copy(x_hbm, xv, lsem.at[CH])
    x_cp.start()

    bar = pltpu.get_barrier_semaphore()
    partner = (node, yy * 2 + (1 - core))
    y_peers = [(node, lax.rem(yy + r, ny) * 2 + core) for r in range(1, ny)]
    n_peers = [(lax.rem(node + r, nn), dp) for r in range(1, nn)]
    for peer in [partner] + y_peers + n_peers:
        pl.semaphore_signal(bar, inc=1, device_id=peer, device_id_type=MESH)
    pl.semaphore_wait(bar, 1 + len(y_peers) + len(n_peers))

    def remote(src, dst, s, r, peer):
        cp = pltpu.make_async_remote_copy(
            src_ref=src, dst_ref=dst, send_sem=s, recv_sem=r,
            device_id=peer, device_id_type=MESH,
        )
        cp.start()
        return cp

    class Reduce:
        def __init__(self, which, out, chunks):
            self.w, self.out, self.chunks = which, out, chunks
            self.rs, self.ys, self.ag = {}, {}, {}

        def rows(self, i, c):
            base, h = self.chunks[i]
            return pl.ds(pl.multiple_of(base + c * h, 8), h)

        def lrows(self, i):
            base, h = self.chunks[i]
            return pl.ds(base // 2, h)

        def start(self, i):
            w = self.w
            self.rs[i] = remote(
                part.at[w, self.rows(i, 1 - core)], land_c.at[w, self.lrows(i)],
                ssem.at[w, 0, i], rsem.at[w, 0, i], partner,
            )

        def across(self, i):
            w = self.w
            self.rs[i].wait_recv()
            mine = self.rows(i, core)
            part[w, mine] = part[w, mine] + land_c[w, self.lrows(i)]
            self.ys[i] = [
                remote(
                    part.at[w, mine], land_y.at[w, r, self.lrows(i)],
                    ssem.at[w, 1 + r, i], rsem.at[w, 1 + r, i], peer,
                )
                for r, peer in enumerate(y_peers)
            ]

        def back(self, i):
            w = self.w
            mine = self.rows(i, core)
            total = part[w, mine]
            for r, cp in enumerate(self.ys[i]):
                cp.wait_recv()
                total = total + land_y[w, r, self.lrows(i)]
            self.out[mine] = total
            self.ag[i] = remote(
                self.out.at[mine], self.out.at[mine],
                ssem.at[w, ny, i], rsem.at[w, ny, i], partner,
            )

        def finish(self, i):
            self.ag[i].wait_recv()

        def drain(self):
            for i in self.rs:
                self.rs[i].wait_send()
                for cp in self.ys[i]:
                    cp.wait_send()
                self.ag[i].wait_send()

    plain = [(i * tk, half) for i in range(CH)]

    red = Reduce(0, cent, plain + [(kk, extra)])
    w = w_ref[...]
    hi, lo = split(w)
    wh[...] = hi
    wl[...] = lo
    part[0, pl.ds(kk, 2 * extra)] = jnp.broadcast_to(
        0.015 * jnp.sum(w, axis=0, keepdims=True), (2 * extra, d)
    )
    red.start(CH)
    for i in range(CH):
        rows = pl.ds(i * tk, tk)
        b_cp[i].wait()
        hi, lo = split(bv[rows])
        bh[rows] = hi
        bl[rows] = lo
        part[0, rows] = dot3(hi, lo, wh[...], wl[...])
        red.start(i)
    order = [CH] + list(range(CH))
    for i in order:
        red.across(i)
    x_cp.wait()

    def split_x(t, _):
        rows = pl.ds(pl.multiple_of(t * VC, VC), VC)
        h, l = split(xv[rows])
        xh[rows] = h
        xl[rows] = l
        return 0

    lax.fori_loop(0, nv // VC, split_x, 0)

    def turn(t, _):
        rows = pl.ds(pl.multiple_of(t * 128, 128), 128)
        h, l = split(jnp.transpose(bv[:, rows]))
        bth[rows] = h
        btl[rows] = l
        return 0

    lax.fori_loop(0, mm // 128, turn, 0)
    for i in order:
        red.back(i)
    for i in order:
        red.finish(i)
    red.drain()

    c0 = cent[pl.ds(kk, 1)]
    for i in range(CH):
        rows = pl.ds(i * tk, tk)
        c = cent[rows]
        bias[rows] = -0.125 * jnp.sum(c * c, axis=1, keepdims=True)
        hi, lo = split(0.25 * (c - c0))
        wh[rows] = hi
        wl[rows] = lo

    nj = nv // VC

    def scores(j, _):
        cols = pl.ds(pl.multiple_of(j * VC, VC), VC)
        top = None
        for i in range(CH):
            rows = pl.ds(i * tk, tk)
            s = dot3(wh[rows], wl[rows], xh[cols], xl[cols], True) + bias[rows]
            ex[rows, cols] = s
            m = jnp.max(s, axis=0, keepdims=True)
            top = m if top is None else jnp.maximum(top, m)
        tot = jnp.zeros_like(top)
        for i in range(CH):
            rows = pl.ds(i * tk, tk)
            e = jnp.exp(ex[rows, cols] - top)
            ex[rows, cols] = e
            tot = tot + jnp.sum(e, axis=0, keepdims=True)
        st[pl.ds(j, 1)] = top
        st[pl.ds(nj + j, 1)] = tot
        return 0

    lax.fori_loop(0, nj, scores, 0)
    st_cp = [
        remote(st, st_in.at[r], st_s.at[r], st_r.at[r], peer)
        for r, peer in enumerate(n_peers)
    ]
    mine = st[pl.ds(0, nj)]
    top, tot = mine, st[pl.ds(nj, nj)]
    for r, cp in enumerate(st_cp):
        cp.wait_recv()
        m, t = st_in[r, pl.ds(0, nj)], st_in[r, pl.ds(nj, nj)]
        new = jnp.maximum(top, m)
        tot = tot * jnp.exp(top - new) + t * jnp.exp(m - new)
        top = new
    fac[...] = jnp.exp(mine - top) / tot

    red2 = Reduce(1, nc, plain)
    for i in range(CH):
        rows = pl.ds(i * tk, tk)

        def terms(j, carry):
            acc, rs = carry
            cols = pl.ds(pl.multiple_of(j * VC, VC), VC)
            r = ex[rows, cols] * fac[pl.ds(j, 1)]
            h, l = split(r)
            acc = acc + dot3(h, l, xh[cols], xl[cols])
            for q in range(VC // 128):
                rs = rs + r[:, q * 128:(q + 1) * 128]
            return acc, rs

        acc, rs = lax.fori_loop(
            0, nj, terms, (jnp.zeros((tk, d), f32), jnp.zeros((tk, 128), f32))
        )
        part[1, rows] = jnp.sum(rs, axis=1, keepdims=True) * cent[rows] - acc
        red2.start(i)
    for i in range(CH):
        red2.across(i)
    for i in range(CH):
        red2.back(i)
    for i in range(CH):
        red2.finish(i)
        rows = pl.ds(i * tk, tk)
        hi, lo = split(nc[rows])
        wh[rows] = hi
        wl[rows] = lo
    red2.drain()

    def gradient(t, _):
        rows = pl.ds(pl.multiple_of(t * 256, 256), 256)
        grad[rows] = dot3(bth[rows], btl[rows], wh[...], wl[...])
        return 0

    h1 = lx1.shape[0]
    p1 = lz1.shape[1]
    p2 = lz2.shape[1]
    g2 = 2 * h1
    other_x = (zz * 2 + (1 - xx), dp)
    z_to = [lax.rem(zz + r, nz) for r in range(1, nz)]
    z_dev = [(t * 2 + xx, dp) for t in z_to]
    sems = iter(range(g_s.shape[0]))
    sent = []

    def ship(src, dst, peer):
        q = next(sems)
        cp = remote(src, dst, g_s.at[q], g_r.at[q], peer)
        sent.append(cp)
        return cp

    def at(start, size):
        return pl.ds(pl.multiple_of(start, 8), size)

    def update(rows, g):
        nw[rows] = shrink * w_ref[rows] - rate * g

    lax.fori_loop(0, mm // 256, gradient, 0)
    a1 = ship(grad.at[at((1 - xx) * h1, h1)], lx1, other_x)
    b1 = [
        ship(grad.at[at(g2 + t * p2, p2)], lz2.at[r], dev)
        for r, (t, dev) in enumerate(zip(z_to, z_dev))
    ]
    keep1 = at(xx * h1, h1)
    a1.wait_recv()
    grad[keep1] = grad[keep1] + lx1[...]
    a2 = [
        ship(grad.at[at(xx * h1 + t * p1, p1)], lz1.at[r], dev)
        for r, (t, dev) in enumerate(zip(z_to, z_dev))
    ]
    own2 = at(g2 + zz * p2, p2)
    total = grad[own2]
    for r, cp in enumerate(b1):
        cp.wait_recv()
        total = total + lz2[r]
    grad[own2] = total
    b2 = ship(grad.at[own2], lx2, other_x)
    own1 = at(xx * h1 + zz * p1, p1)
    total = grad[own1]
    for r, cp in enumerate(a2):
        cp.wait_recv()
        total = total + lz1[r]
    update(own1, total)
    a3 = [ship(nw.at[own1], nw.at[own1], dev) for dev in z_dev]
    b2.wait_recv()
    update(own2, grad[own2] + lx2[...])
    b3 = [ship(nw.at[own2], nw.at[own2], dev) for dev in z_dev]
    for cp in a3:
        cp.wait_recv()
    a4 = ship(nw.at[keep1], nw.at[keep1], other_x)
    for cp in b3:
        cp.wait_recv()
    a4.wait_recv()
    nw_cp = pltpu.make_async_copy(nw, nw_hbm, lsem.at[0])
    nw_cp.start()
    hi, lo = split(nw[...])
    wh[...] = hi
    wl[...] = lo

    red3 = Reduce(2, cent, plain)
    for i in range(CH):
        rows = pl.ds(i * tk, tk)
        part[2, rows] = dot3(bh[rows], bl[rows], wh[...], wl[...])
        red3.start(i)
    for i in range(CH):
        red3.across(i)
    for i in range(CH):
        red3.back(i)
    out_cp = []
    for i in range(CH):
        red3.finish(i)
        rows = pl.ds(i * tk, tk)
        cp = pltpu.make_async_copy(cent.at[rows], nc_hbm.at[rows], lsem.at[1 + i])
        cp.start()
        out_cp.append(cp)
    red3.drain()
    for cp in sent + st_cp:
        cp.wait_send()
    nw_cp.wait()
    for cp in out_cp:
        cp.wait()


def body(samples, basis_matrix, weights):
    nn, nd = lax.axis_size("nodes"), lax.axis_size("dp")
    nv, d = samples.shape
    kk, mm = basis_matrix.shape
    rate = 8.0 * math.sqrt(kk * nn) / (nv * nd)
    ny, nz = nd // 2, nn // 2
    nj = nv // VC
    h1 = mm // 4
    n_ship = 3 + 4 * (nz - 1)
    vm = pltpu.VMEM
    dma = pltpu.SemaphoreType.DMA
    anyspec = pl.BlockSpec(memory_space=pl.ANY)
    return pl.pallas_call(
        functools.partial(kernel, nn, nd, rate),
        out_shape=(
            jax.ShapeDtypeStruct((mm, d), f32),
            jax.ShapeDtypeStruct((kk, d), f32),
        ),
        in_specs=[anyspec, anyspec, pl.BlockSpec(memory_space=pltpu.VMEM)],
        out_specs=(anyspec, anyspec),
        scratch_shapes=[
            vm((nv, d), f32), vm((kk, mm), f32),
            vm((nv, d), bf16), vm((nv, d), bf16),
            vm((kk, mm), bf16), vm((kk, mm), bf16),
            vm((mm, kk), bf16), vm((mm, kk), bf16),
            vm((max(kk, mm), d), bf16), vm((max(kk, mm), d), bf16),
            vm((3, kk + 16, d), f32), vm((kk + 16, d), f32),
            vm((3, kk // 2 + 8, d), f32), vm((3, ny - 1, kk // 2 + 8, d), f32),
            vm((kk, 1), f32), vm((kk, nv), f32),
            vm((2 * nj, VC), f32), vm((nn - 1, 2 * nj, VC), f32), vm((nj, VC), f32),
            vm((mm, d), f32),
            vm((h1, d), f32), vm((nz - 1, h1 // nz, d), f32),
            vm((2 * h1 // nz, d), f32), vm((nz - 1, 2 * h1 // nz, d), f32),
            vm((mm, d), f32), vm((kk, d), f32),
            dma((CH + 1,)),
            dma((3, ny + 1, CH + 1)), dma((3, ny + 1, CH + 1)),
            dma((nn - 1,)), dma((nn - 1,)),
            dma((n_ship,)), dma((n_ship,)),
        ],
        compiler_params=pltpu.CompilerParams(
            collective_id=0, has_side_effects=True, vmem_limit_bytes=64000000
        ),
    )(samples, basis_matrix, weights)


def solution(mesh):
    in_specs = (P("dp", None), P("nodes", "dp"), P("dp", None))
    out_specs = (P("dp", None), P("nodes", None))
    return jax.shard_map(body, mesh=mesh, in_specs=in_specs, out_specs=out_specs, check_vma=False)
```

time: 351 us -> 134 us (0.38)
  waiting for transfers between devices: 201 us -> 0 us
  Pallas kernels: 0 us -> 127 us
  matrix products: 58.4 us -> 0 us
  blocking collectives: 48.6 us -> 0 us
  other arithmetic: 16.3 us -> 0 us
  between operations: 13.9 us -> 0.64 us
  local copies, waits for them, and re-layouts: 11.3 us -> 4.52 us
    psum x4 -> x0, waiting for transfers between devices: 201 us -> none  [the longest x1 78.6 us: body(): gradient = lax.psum(partial_gradient, 'nodes')]
    pallas_call x0 -> x1, Pallas kernels: none -> 127 us  [body(): pl.pallas_call(functools.partial(kernel, nn, nd, rate), out_shape=(jax.Sh...]
    dot_general x5 -> x0, matrix products: 58.4 us -> none  [the longest x1 20.6 us: body(): jnp.dot(resp, samples, precision=highest, preferred_element_type=jnp.floa...]
    all_gather x2 -> x0, blocking collectives: 48.6 us -> none  [merged_2(): gathered = jax.tree.map(lambda a: lax.all_gather(a, axis), part)]
    reduce_sum x3 -> x0, other arithmetic: 14.7 us -> none  [the longest x1 9.46 us: body(): local_terms = jnp.sum(resp, axis=1)[:, None] * centres - weighted]
    unnamed x11 -> x2, local copies, waits for them, and re-layouts: 11.1 us -> 4.52 us
  transfers between devices with their start and end apart: 4 -> 0, of which waited for: 4 -> 0; matrix products, arithmetic and copies ran while one was open for 0% -> 0% of each run, Pallas kernels for 0% -> 0%
where the time goes in v1:
time: 134 us; the launch traced here: 132 us
  Pallas kernels  127 us (95%)
  local copies, waits for them, and re-layouts  4.52 us (3%)
    pallas_call x1, Pallas kernels, body(): pl.pallas_call(functools.partial(kernel, nn, nd, rate), out_shape=(jax.Sh...  127 us
    unnamed x2, local copies, waits for them, and re-layouts  4.52 us

profile of v1, /device:TPU:1, one launch (start us, length us, event | category | flops | bytes accessed | tf_op | source)
XLA Modules:
  0.0 132.2 jit_solution(7436442015292615051)
XLA Ops:
  0.6 127.0 %shard_map.50 = (f32[1024,256]{1,0:T(8,128)}, f32[1024,256]{1,0:T(8,128)}) custom-call(f32[4096,256]{1,0:T(8,128)} %x_hbm.1, f32[1024,1024]{1,0:T(8,128)} %b_hbm.1, f32[1024,256]{1,0:T(8,128)} %w_ref.1), custom_call_target="tpu_custom_call" | custom-call | tf_op jit(solution)/shard_map/pallas_call | solution.py:365
  127.6 2.3 %copy.7 = f32[1024,256]{1,0:T(8,128)} copy(f32[1024,256]{1,0:T(8,128)} %get-tuple-element.4) | data formatting | bytes 2097152
  129.9 2.3 %copy.8 = f32[1024,256]{1,0:T(8,128)} copy(f32[1024,256]{1,0:T(8,128)} %get-tuple-element.5) | data formatting | bytes 2097152

commit v2 on v1

--- a/solution.py
+++ b/solution.py
@@ -32,12 +32,13 @@
 
 def kernel(
     nn, nd, rate,
-    x_hbm, b_hbm, w_ref, nw_hbm, nc_hbm,
-    xv, bv, xh, xl, bh, bl, bth, btl, wh, wl,
+    x_hbm, b_hbm, w_hbm, nw_hbm, nc_hbm,
+    w_ref, xv, bv, xh, xl, bh, bl, bth, btl, wh, wl,
     part, cent, land_c, land_y,
     bias, ex, st, st_in, fac,
-    grad, lx1, lz1, lx2, lz2, nw, nc,
-    lsem, ssem, rsem, st_s, st_r, g_s, g_r,
+    grad, lx1, lx2, lz2, nw, nc,
+    lin, lmid,
+    lsem, ssem, rsem, st_s, st_r, g_s, g_r, c_s, c_r,
 ):
     kk, mm = bv.shape
     nv, d = xv.shape
@@ -53,6 +54,8 @@
     half = tk // 2
     extra = 8
 
+    w_cp = pltpu.make_async_copy(w_hbm, w_ref, lsem.at[CH + 1])
+    w_cp.start()
     b_cp = []
     for i in range(CH):
         rows = pl.ds(i * tk, tk)
@@ -137,6 +140,7 @@
     plain = [(i * tk, half) for i in range(CH)]
 
     red = Reduce(0, cent, plain + [(kk, extra)])
+    w_cp.wait()
     w = w_ref[...]
     hi, lo = split(w)
     wh[...] = hi
@@ -153,9 +157,9 @@
         bl[rows] = lo
         part[0, rows] = dot3(hi, lo, wh[...], wl[...])
         red.start(i)
+        red.across(CH if i == 0 else i - 1)
     order = [CH] + list(range(CH))
-    for i in order:
-        red.across(i)
+    red.across(CH - 1)
     x_cp.wait()
 
     def split_x(t, _):
@@ -245,8 +249,9 @@
         )
         part[1, rows] = jnp.sum(rs, axis=1, keepdims=True) * cent[rows] - acc
         red2.start(i)
-    for i in range(CH):
-        red2.across(i)
+        if i:
+            red2.across(i - 1)
+    red2.across(CH - 1)
     for i in range(CH):
         red2.back(i)
     for i in range(CH):
@@ -257,15 +262,22 @@
         wl[rows] = lo
     red2.drain()
 
-    def gradient(t, _):
-        rows = pl.ds(pl.multiple_of(t * 256, 256), 256)
+    def gradient(start, size):
+        rows = pl.ds(start, size)
         grad[rows] = dot3(bth[rows], btl[rows], wh[...], wl[...])
-        return 0
-
-    h1 = lx1.shape[0]
-    p1 = lz1.shape[1]
+
+    nc1, hc = lx1.shape[0], lx1.shape[1]
     p2 = lz2.shape[1]
-    g2 = 2 * h1
+    g2 = nc1 * 2 * hc
+    mid = nz // 2
+    left = zz < mid
+    is_mid = jnp.logical_or(zz == mid - 1, zz == mid)
+    not_mid = jnp.logical_not(is_mid)
+    is_end = jnp.logical_or(zz == 0, zz == nz - 1)
+    not_end = jnp.logical_not(is_end)
+    step = jnp.where(left, 1, -1)
+    inner = (lax.rem(zz + step + nz, nz) * 2 + xx, dp)
+    outer = (lax.rem(zz - step + nz, nz) * 2 + xx, dp)
     other_x = (zz * 2 + (1 - xx), dp)
     z_to = [lax.rem(zz + r, nz) for r in range(1, nz)]
     z_dev = [(t * 2 + xx, dp) for t in z_to]
@@ -284,42 +296,108 @@
     def update(rows, g):
         nw[rows] = shrink * w_ref[rows] - rate * g
 
-    lax.fori_loop(0, mm // 256, gradient, 0)
-    a1 = ship(grad.at[at((1 - xx) * h1, h1)], lx1, other_x)
+    def plan(src, dst, kind, c, peer):
+        return pltpu.make_async_remote_copy(
+            src_ref=src, dst_ref=dst, send_sem=c_s.at[kind, c], recv_sem=c_r.at[kind, c],
+            device_id=peer, device_id_type=MESH,
+        )
+
+    gradient(g2, mm - g2)
     b1 = [
         ship(grad.at[at(g2 + t * p2, p2)], lz2.at[r], dev)
         for r, (t, dev) in enumerate(zip(z_to, z_dev))
     ]
-    keep1 = at(xx * h1, h1)
-    a1.wait_recv()
-    grad[keep1] = grad[keep1] + lx1[...]
-    a2 = [
-        ship(grad.at[at(xx * h1 + t * p1, p1)], lz1.at[r], dev)
-        for r, (t, dev) in enumerate(zip(z_to, z_dev))
-    ]
+    keep = [at((2 * c + xx) * hc, hc) for c in range(nc1)]
+    give = [at((2 * c + 1 - xx) * hc, hc) for c in range(nc1)]
+    x_rs, x_ag = [], {}
+    inward = [plan(grad.at[keep[c]], lin.at[c], 0, c, inner) for c in range(nc1)]
+    swap = [plan(grad.at[keep[c]], lmid.at[c], 1, c, inner) for c in range(nc1)]
+    outward = [plan(nw.at[keep[c]], nw.at[keep[c]], 2, c, outer) for c in range(nc1)]
+    for c in range(nc1):
+        gradient(2 * c * hc, 2 * hc)
+        x_rs.append(ship(grad.at[give[c]], lx1.at[c], other_x))
+
+    def stage0(c):
+        x_rs[c].wait_recv()
+        grad[keep[c]] = grad[keep[c]] + lx1[c]
+
+        @pl.when(jnp.logical_and(is_end, not_mid))
+        def _():
+            inward[c].start()
+
+    def stage1(c):
+        @pl.when(not_end)
+        def _():
+            inward[c].wait_recv()
+            grad[keep[c]] = grad[keep[c]] + lin[c]
+
+        @pl.when(jnp.logical_and(not_end, not_mid))
+        def _():
+            inward[c].start()
+
+        @pl.when(is_mid)
+        def _():
+            swap[c].start()
+
+    def stage2(c):
+        @pl.when(is_mid)
+        def _():
+            swap[c].wait_recv()
+            update(keep[c], grad[keep[c]] + lmid[c])
+
+        @pl.when(jnp.logical_and(is_mid, not_end))
+        def _():
+            outward[c].start()
+
+    def stage3(c):
+        @pl.when(not_mid)
+        def _():
+            outward[c].wait_recv()
+
+        @pl.when(jnp.logical_and(not_mid, not_end))
+        def _():
+            outward[c].start()
+
+        x_ag[c] = ship(nw.at[keep[c]], nw.at[keep[c]], other_x)
+
     own2 = at(g2 + zz * p2, p2)
-    total = grad[own2]
-    for r, cp in enumerate(b1):
-        cp.wait_recv()
-        total = total + lz2[r]
-    grad[own2] = total
-    b2 = ship(grad.at[own2], lx2, other_x)
-    own1 = at(xx * h1 + zz * p1, p1)
-    total = grad[own1]
-    for r, cp in enumerate(a2):
-        cp.wait_recv()
-        total = total + lz1[r]
-    update(own1, total)
-    a3 = [ship(nw.at[own1], nw.at[own1], dev) for dev in z_dev]
-    b2.wait_recv()
-    update(own2, grad[own2] + lx2[...])
-    b3 = [ship(nw.at[own2], nw.at[own2], dev) for dev in z_dev]
-    for cp in a3:
-        cp.wait_recv()
-    a4 = ship(nw.at[keep1], nw.at[keep1], other_x)
+    for t in range(nc1 + 3):
+        if t < nc1:
+            stage0(t)
+        if 0 <= t - 1 < nc1:
+            stage1(t - 1)
+        if 0 <= t - 2 < nc1:
+            stage2(t - 2)
+        if 0 <= t - 3 < nc1:
+            stage3(t - 3)
+        if t == 2:
+            total = grad[own2]
+            for r, cp in enumerate(b1):
+                cp.wait_recv()
+                total = total + lz2[r]
+            grad[own2] = total
+            b2 = ship(grad.at[own2], lx2, other_x)
+        if t == 4:
+            b2.wait_recv()
+            update(own2, grad[own2] + lx2[...])
+            b3 = [ship(nw.at[own2], nw.at[own2], dev) for dev in z_dev]
     for cp in b3:
         cp.wait_recv()
-    a4.wait_recv()
+    for c in range(nc1):
+        x_ag[c].wait_recv()
+
+        @pl.when(not_mid)
+        def _():
+            inward[c].wait_send()
+
+        @pl.when(is_mid)
+        def _():
+            swap[c].wait_send()
+
+        @pl.when(not_end)
+        def _():
+            outward[c].wait_send()
+
     nw_cp = pltpu.make_async_copy(nw, nw_hbm, lsem.at[0])
     nw_cp.start()
     hi, lo = split(nw[...])
@@ -331,8 +409,9 @@
         rows = pl.ds(i * tk, tk)
         part[2, rows] = dot3(bh[rows], bl[rows], wh[...], wl[...])
         red3.start(i)
-    for i in range(CH):
-        red3.across(i)
+        if i:
+            red3.across(i - 1)
+    red3.across(CH - 1)
     for i in range(CH):
         red3.back(i)
     out_cp = []
@@ -357,8 +436,10 @@
     rate = 8.0 * math.sqrt(kk * nn) / (nv * nd)
     ny, nz = nd // 2, nn // 2
     nj = nv // VC
-    h1 = mm // 4
-    n_ship = 3 + 4 * (nz - 1)
+    nc1 = 6
+    hc = mm // 16
+    g2 = mm - 2 * nc1 * hc
+    n_ship = 2 * nc1 + 1 + 2 * (nz - 1)
     vm = pltpu.VMEM
     dma = pltpu.SemaphoreType.DMA
     anyspec = pl.BlockSpec(memory_space=pl.ANY)
@@ -368,10 +449,10 @@
             jax.ShapeDtypeStruct((mm, d), f32),
             jax.ShapeDtypeStruct((kk, d), f32),
         ),
-        in_specs=[anyspec, anyspec, pl.BlockSpec(memory_space=pltpu.VMEM)],
+        in_specs=[anyspec, anyspec, anyspec],
         out_specs=(anyspec, anyspec),
         scratch_shapes=[
-            vm((nv, d), f32), vm((kk, mm), f32),
+            vm((mm, d), f32), vm((nv, d), f32), vm((kk, mm), f32),
             vm((nv, d), bf16), vm((nv, d), bf16),
             vm((kk, mm), bf16), vm((kk, mm), bf16),
             vm((mm, kk), bf16), vm((mm, kk), bf16),
@@ -381,13 +462,13 @@
             vm((kk, 1), f32), vm((kk, nv), f32),
             vm((2 * nj, VC), f32), vm((nn - 1, 2 * nj, VC), f32), vm((nj, VC), f32),
             vm((mm, d), f32),
-            vm((h1, d), f32), vm((nz - 1, h1 // nz, d), f32),
-            vm((2 * h1 // nz, d), f32), vm((nz - 1, 2 * h1 // nz, d), f32),
+            vm((nc1, hc, d), f32), vm((g2 // nz, d), f32), vm((nz - 1, g2 // nz, d), f32),
             vm((mm, d), f32), vm((kk, d), f32),
-            dma((CH + 1,)),
+            vm((nc1, hc, d), f32), vm((nc1, hc, d), f32),
+            dma((CH + 2,)),
             dma((3, ny + 1, CH + 1)), dma((3, ny + 1, CH + 1)),
             dma((nn - 1,)), dma((nn - 1,)),
-            dma((n_ship,)), dma((n_ship,)),
+            dma((n_ship,)), dma((n_ship,)), dma((3, nc1)), dma((3, nc1)),
         ],
         compiler_params=pltpu.CompilerParams(
             collective_id=0, has_side_effects=True, vmem_limit_bytes=64000000

time: 134 us -> 122 us (0.910); the launches traced: 132 us -> 122 us
  Pallas kernels: 127 us -> 117 us
    pallas_call x1, Pallas kernels: 127 us -> 117 us  [body(): pl.pallas_call(functools.partial(kernel, nn, nd, rate), out_shape=(jax.Sh...]
where the time goes in v2:
time: 122 us
  Pallas kernels  117 us (96%)
  local copies, waits for them, and re-layouts  4.52 us (4%)
    pallas_call x1, Pallas kernels, body(): pl.pallas_call(functools.partial(kernel, nn, nd, rate), out_shape=(jax.Sh...  117 us
    unnamed x2, local copies, waits for them, and re-layouts  4.52 us

profile of v2, /device:TPU:1, one launch (start us, length us, event | category | flops | bytes accessed | tf_op | source)
XLA Modules:
  0.0 121.7 jit_solution(13923745820217105764)
XLA Ops:
  0.6 116.6 %shard_map.50 = (f32[1024,256]{1,0:T(8,128)}, f32[1024,256]{1,0:T(8,128)}) custom-call(f32[4096,256]{1,0:T(8,128)} %x_hbm.1, f32[1024,1024]{1,0:T(8,128)} %b_hbm.1, f32[1024,256]{1,0:T(8,128)} %w_hbm.1), custom_call_target="tpu_custom_call" | custom-call | tf_op jit(solution)/shard_map/pallas_call | solution.py:446
  117.2 2.3 %copy.7 = f32[1024,256]{1,0:T(8,128)} copy(f32[1024,256]{1,0:T(8,128)} %get-tuple-element.4) | data formatting | bytes 2097152
  119.5 2.3 %copy.8 = f32[1024,256]{1,0:T(8,128)} copy(f32[1024,256]{1,0:T(8,128)} %get-tuple-element.5) | data formatting | bytes 2097152

commit v3 on v2

--- a/solution.py
+++ b/solution.py
@@ -14,6 +14,8 @@
 shrink = 0.95
 CH = 4
 VC = 512
+LAG = 2
+EARLY = 2
 
 
 def split(a):
@@ -37,7 +39,7 @@
     part, cent, land_c, land_y,
     bias, ex, st, st_in, fac,
     grad, lx1, lx2, lz2, nw, nc,
-    lin, lmid,
+    lin, lmid, rsum,
     lsem, ssem, rsem, st_s, st_r, g_s, g_r, c_s, c_r,
 ):
     kk, mm = bv.shape
@@ -71,7 +73,6 @@
     n_peers = [(lax.rem(node + r, nn), dp) for r in range(1, nn)]
     for peer in [partner] + y_peers + n_peers:
         pl.semaphore_signal(bar, inc=1, device_id=peer, device_id_type=MESH)
-    pl.semaphore_wait(bar, 1 + len(y_peers) + len(n_peers))
 
     def remote(src, dst, s, r, peer):
         cp = pltpu.make_async_remote_copy(
@@ -148,7 +149,6 @@
     part[0, pl.ds(kk, 2 * extra)] = jnp.broadcast_to(
         0.015 * jnp.sum(w, axis=0, keepdims=True), (2 * extra, d)
     )
-    red.start(CH)
     for i in range(CH):
         rows = pl.ds(i * tk, tk)
         b_cp[i].wait()
@@ -156,6 +156,9 @@
         bh[rows] = hi
         bl[rows] = lo
         part[0, rows] = dot3(hi, lo, wh[...], wl[...])
+        if i == 0:
+            pl.semaphore_wait(bar, 1 + len(y_peers) + len(n_peers))
+            red.start(CH)
         red.start(i)
         red.across(CH if i == 0 else i - 1)
     order = [CH] + list(range(CH))
@@ -194,10 +197,10 @@
         wh[rows] = hi
         wl[rows] = lo
 
-    nj = nv // VC
-
-    def scores(j, _):
-        cols = pl.ds(pl.multiple_of(j * VC, VC), VC)
+    njh = st.shape[1] // 2
+
+    def scores(g, j):
+        cols = pl.ds(pl.multiple_of((g * njh + j) * VC, VC), VC)
         top = None
         for i in range(CH):
             rows = pl.ds(i * tk, tk)
@@ -211,42 +214,62 @@
             e = jnp.exp(ex[rows, cols] - top)
             ex[rows, cols] = e
             tot = tot + jnp.sum(e, axis=0, keepdims=True)
-        st[pl.ds(j, 1)] = top
-        st[pl.ds(nj + j, 1)] = tot
-        return 0
-
-    lax.fori_loop(0, nj, scores, 0)
-    st_cp = [
-        remote(st, st_in.at[r], st_s.at[r], st_r.at[r], peer)
-        for r, peer in enumerate(n_peers)
-    ]
-    mine = st[pl.ds(0, nj)]
-    top, tot = mine, st[pl.ds(nj, nj)]
-    for r, cp in enumerate(st_cp):
-        cp.wait_recv()
-        m, t = st_in[r, pl.ds(0, nj)], st_in[r, pl.ds(nj, nj)]
-        new = jnp.maximum(top, m)
-        tot = tot * jnp.exp(top - new) + t * jnp.exp(m - new)
-        top = new
-    fac[...] = jnp.exp(mine - top) / tot
+        st[g, pl.ds(j, 1)] = top
+        st[g, pl.ds(njh + j, 1)] = tot
+
+    st_cp = []
+    for g in range(2):
+
+        def scores_g(j, _):
+            scores(g, j)
+            return 0
+
+        lax.fori_loop(0, njh, scores_g, 0)
+        st_cp += [
+            remote(st.at[g], st_in.at[g, r], st_s.at[g, r], st_r.at[g, r], peer)
+            for r, peer in enumerate(n_peers)
+        ]
+
+    def merge(g):
+        mine = st[g, pl.ds(0, njh)]
+        top, tot = mine, st[g, pl.ds(njh, njh)]
+        for r in range(nn - 1):
+            st_cp[g * (nn - 1) + r].wait_recv()
+            m, t = st_in[g, r, pl.ds(0, njh)], st_in[g, r, pl.ds(njh, njh)]
+            new = jnp.maximum(top, m)
+            tot = tot * jnp.exp(top - new) + t * jnp.exp(m - new)
+            top = new
+        fac[g] = jnp.exp(mine - top) / tot
 
     red2 = Reduce(1, nc, plain)
-    for i in range(CH):
-        rows = pl.ds(i * tk, tk)
-
-        def terms(j, carry):
+
+    def terms(i, g, start):
+        rows = pl.ds(i * tk, tk)
+
+        def one(j, carry):
             acc, rs = carry
-            cols = pl.ds(pl.multiple_of(j * VC, VC), VC)
-            r = ex[rows, cols] * fac[pl.ds(j, 1)]
+            cols = pl.ds(pl.multiple_of((g * njh + j) * VC, VC), VC)
+            r = ex[rows, cols] * fac[g, pl.ds(j, 1)]
             h, l = split(r)
             acc = acc + dot3(h, l, xh[cols], xl[cols])
             for q in range(VC // 128):
                 rs = rs + r[:, q * 128:(q + 1) * 128]
             return acc, rs
 
-        acc, rs = lax.fori_loop(
-            0, nj, terms, (jnp.zeros((tk, d), f32), jnp.zeros((tk, 128), f32))
-        )
+        return lax.fori_loop(0, njh, one, start, unroll=2)
+
+    zero = (jnp.zeros((tk, d), f32), jnp.zeros((tk, 128), f32))
+    merge(0)
+    for i in range(EARLY):
+        rows = pl.ds(i * tk, tk)
+        acc, rs = terms(i, 0, zero)
+        grad[rows] = acc
+        rsum[rows] = rs
+    merge(1)
+    for i in range(CH):
+        rows = pl.ds(i * tk, tk)
+        first = (grad[rows], rsum[rows]) if i < EARLY else terms(i, 0, zero)
+        acc, rs = terms(i, 1, first)
         part[1, rows] = jnp.sum(rs, axis=1, keepdims=True) * cent[rows] - acc
         red2.start(i)
         if i:
@@ -361,23 +384,18 @@
         x_ag[c] = ship(nw.at[keep[c]], nw.at[keep[c]], other_x)
 
     own2 = at(g2 + zz * p2, p2)
-    for t in range(nc1 + 3):
-        if t < nc1:
-            stage0(t)
-        if 0 <= t - 1 < nc1:
-            stage1(t - 1)
-        if 0 <= t - 2 < nc1:
-            stage2(t - 2)
-        if 0 <= t - 3 < nc1:
-            stage3(t - 3)
-        if t == 2:
+    for t in range(nc1 + 3 * LAG):
+        for n, stage in enumerate((stage0, stage1, stage2, stage3)):
+            if 0 <= t - n * LAG < nc1:
+                stage(t - n * LAG)
+        if t == 3:
             total = grad[own2]
             for r, cp in enumerate(b1):
                 cp.wait_recv()
                 total = total + lz2[r]
             grad[own2] = total
             b2 = ship(grad.at[own2], lx2, other_x)
-        if t == 4:
+        if t == 6:
             b2.wait_recv()
             update(own2, grad[own2] + lx2[...])
             b3 = [ship(nw.at[own2], nw.at[own2], dev) for dev in z_dev]
@@ -460,14 +478,14 @@
             vm((3, kk + 16, d), f32), vm((kk + 16, d), f32),
             vm((3, kk // 2 + 8, d), f32), vm((3, ny - 1, kk // 2 + 8, d), f32),
             vm((kk, 1), f32), vm((kk, nv), f32),
-            vm((2 * nj, VC), f32), vm((nn - 1, 2 * nj, VC), f32), vm((nj, VC), f32),
-            vm((mm, d), f32),
+            vm((2, nj, VC), f32), vm((2, nn - 1, nj, VC), f32), vm((2, nj // 2, VC), f32),
+            vm((max(mm, kk), d), f32),
             vm((nc1, hc, d), f32), vm((g2 // nz, d), f32), vm((nz - 1, g2 // nz, d), f32),
             vm((mm, d), f32), vm((kk, d), f32),
-            vm((nc1, hc, d), f32), vm((nc1, hc, d), f32),
+            vm((nc1, hc, d), f32), vm((nc1, hc, d), f32), vm((kk, 128), f32),
             dma((CH + 2,)),
             dma((3, ny + 1, CH + 1)), dma((3, ny + 1, CH + 1)),
-            dma((nn - 1,)), dma((nn - 1,)),
+            dma((2, nn - 1)), dma((2, nn - 1)),
             dma((n_ship,)), dma((n_ship,)), dma((3, nc1)), dma((3, nc1)),
         ],
         compiler_params=pltpu.CompilerParams(

time: 122 us -> 112 us (0.918)
  Pallas kernels: 117 us -> 107 us
    pallas_call x1, Pallas kernels: 117 us -> 107 us  [body(): pl.pallas_call(functools.partial(kernel, nn, nd, rate), out_shape=(jax.Sh...]
where the time goes in v3:
time: 112 us
  Pallas kernels  107 us (96%)
  local copies, waits for them, and re-layouts  4.52 us (4%)
    pallas_call x1, Pallas kernels, body(): pl.pallas_call(functools.partial(kernel, nn, nd, rate), out_shape=(jax.Sh...  107 us
    unnamed x2, local copies, waits for them, and re-layouts  4.52 us

profile of v3, /device:TPU:1, one launch (start us, length us, event | category | flops | bytes accessed | tf_op | source)
XLA Modules:
  0.0 112.1 jit_solution(15736746885707552546)
XLA Ops:
  0.6 106.9 %shard_map.50 = (f32[1024,256]{1,0:T(8,128)}, f32[1024,256]{1,0:T(8,128)}) custom-call(f32[4096,256]{1,0:T(8,128)} %x_hbm.1, f32[1024,1024]{1,0:T(8,128)} %b_hbm.1, f32[1024,256]{1,0:T(8,128)} %w_hbm.1), custom_call_target="tpu_custom_call" | custom-call | tf_op jit(solution)/shard_map/pallas_call | solution.py:464
  107.6 2.3 %copy.7 = f32[1024,256]{1,0:T(8,128)} copy(f32[1024,256]{1,0:T(8,128)} %get-tuple-element.4) | data formatting | bytes 2097152
  109.8 2.3 %copy.8 = f32[1024,256]{1,0:T(8,128)} copy(f32[1024,256]{1,0:T(8,128)} %get-tuple-element.5) | data formatting | bytes 2097152
